TPU v7x, 32 devices: a whole 2x2x4 slice. The times are simulated.
32 devices in a mesh: grp: 2 (over x), col: 16 (over z, y, core).
Axes of the slice: x: 2, y: 2, z: 4, core: 2. Of those that a mesh axis runs over, the one named last changes fastest.
Arguments:
- database: int32 [256, 4096], P('col', 'grp'), parts along dimension 1, may hold values from 0 to 255
- queries: int32 [16, 256], P('grp', 'col'), parts along dimension 0, may hold values from -2147483648 to 2147483646
- key_rows: int32 [16, 8192], P('grp', 'col'), parts along dimension 0, may hold values from -2147483648 to 2147483646
- hint: int32 [4, 1024], P('grp'), parts along dimension 0, may hold values from -2147483648 to 2147483646
- assignment: int32 [32], P('grp'), parts along dimension 0, may hold values from 0 to 15, each once
Outputs:
- packed: float32 [32, 2, 1024], P(('grp', 'col')), parts along dimension 0
There are 2 independent parts, one for each index of `grp`. A program takes and returns all parts, laid end to end along the dimension named above; each array names one. Nothing has to cross between parts.
Inputs may be any that keep to these rules, and one draw needn't show every extreme that they name: `assignment`: every unit appears in exactly one slot.
All inputs are finite; a program needn't handle non-finite values.
Results may differ from a plain program's by a relative error of at most 0.0003.
Values sent between devices are 32-bit elements; how exact they have to be, the bound alone decides.
A program may use at most 128 MiB of HBM per device.

v0:
```python
import jax
import jax.numpy as jnp
from jax import lax
from jax.sharding import PartitionSpec as P

LEVELS = 2
DIGITS = 2


def automorph(polynomial, galois):
    cycle_width = polynomial.shape[0]
    inverse = pow(galois, -1, 2 * cycle_width)
    source = jnp.arange(cycle_width, dtype=jnp.int32) * inverse % (2 * cycle_width)
    picked = jnp.take(polynomial, source % cycle_width, axis=0)
    return jnp.where(source < cycle_width, picked, -picked)


def toeplitz(key_poly):
    cycle_width = key_poly.shape[0]
    shifted = jnp.concatenate([-key_poly[1:], key_poly, -key_poly[:1]])
    tiled_rows = jnp.tile(shifted, cycle_width)[: cycle_width * (2 * cycle_width - 1)]
    return tiled_rows.reshape(cycle_width, 2 * cycle_width - 1)[
        :, cycle_width - 1 : 2 * cycle_width - 1
    ]


def switch_section(mask_poly, value_poly, section_keys, galois):
    cycle_width = mask_poly.shape[0]
    rotated_mask = automorph(mask_poly, galois)
    rotated_value = automorph(value_poly, galois)
    switched = jnp.zeros((2 * cycle_width,), jnp.int32)
    for digit_index in range(section_keys.shape[0]):
        digit_row = jnp.bitwise_and(jnp.right_shift(rotated_mask, 16 * digit_index), 65535)
        matrix = jnp.concatenate(
            [toeplitz(section_keys[digit_index, 0]), toeplitz(section_keys[digit_index, 1])], axis=1
        )
        switched = (
            switched + jnp.dot(digit_row[None, :], matrix, preferred_element_type=jnp.int32)[0]
        )
    return (mask_poly + switched[:cycle_width], value_poly + rotated_value + switched[cycle_width:])


def pack_unit(mask_poly, value_poly, key_row):
    cycle_width = mask_poly.shape[0]
    section_table = key_row.reshape(LEVELS, DIGITS, 2, cycle_width)
    for section_index in range(LEVELS):
        galois = cycle_width // 2**section_index + 1
        mask_poly, value_poly = switch_section(
            mask_poly, value_poly, section_table[section_index], galois
        )
    return jnp.stack([mask_poly, value_poly])


def split_words(words):
    lower_half = jnp.bitwise_and(words, 65535).astype(jnp.float32)
    upper_half = jnp.bitwise_and(jnp.right_shift(words, 16), 65535).astype(jnp.float32)
    return (lower_half, upper_half)


def join_words(lower_half, upper_half):
    return lower_half.astype(jnp.int32) + jnp.left_shift(upper_half.astype(jnp.int32), 16)


def on_device(database, queries, key_rows, hint, assignment):
    cycle_width = hint.shape[1]
    poly_count = hint.shape[0]
    slot_count = assignment.shape[0] // lax.axis_size("col")
    key_table = lax.all_gather(key_rows, "col", axis=1, tiled=True)
    partial_value = jnp.dot(queries, database, preferred_element_type=jnp.int32)
    owned_slots = lax.dynamic_slice_in_dim(
        assignment, lax.axis_index("col") * slot_count, slot_count
    )
    lower_half, upper_half = split_words(partial_value)
    lower_sum, upper_sum = lax.psum((lower_half, upper_half), "col")
    summed = join_words(lower_sum, upper_sum)
    value_rows = jnp.take(summed.reshape(-1, cycle_width), owned_slots, axis=0)

    def pack_one(inputs):
        unit_index, value_poly = inputs
        client = unit_index // poly_count
        poly_index = unit_index % poly_count
        mask_poly = lax.dynamic_index_in_dim(hint, poly_index, 0, keepdims=False)
        key_row = lax.dynamic_index_in_dim(key_table, client, 0, keepdims=False)
        return pack_unit(mask_poly, value_poly, key_row)

    packed_words = lax.map(pack_one, (owned_slots, value_rows))
    return packed_words.astype(jnp.float32) * 2.0 ** (-32)


def solution(mesh):
    placed = (P("col", "grp"), P("grp", "col"), P("grp", "col"), P("grp", None), P("grp"))
    return jax.shard_map(
        on_device,
        mesh=mesh,
        in_specs=placed,
        out_specs=P(("grp", "col"), None, None),
        check_vma=False,
    )
```

profile of v0, /device:TPU:0, one launch (start us, length us, event | category | flops | bytes accessed | tf_op | source)
XLA Modules:
  0.0 325.9 jit_solution(6749545963673076256)
XLA Ops:
  7.4 1.6 and_convert_fusion.1
  9.1 1.2 dynamic_slice.19
  12.9 24.2 %all_gather.3 = s32[8,8192]{1,0:T(8,128)S(1)} all-gather(s32[8,512]{1,0:T(8,128)} %param.9), channel_id=1, replica_groups=mesh['grp'=2,'col'=16] {'col'}, dimensions={1}, use_global_device_ids=true | all-gather | bytes 278528 | tf_op jit(solution)/shard_map/all_gather | solution.py:68
  40.4 2.0 copy.8
  42.4 3.7 %slice.292 = s32[2096128]{0:T(1024)} slice(s32[2097152]{0:T(1024)S(1)} %bitcast.75), slice={[0:2096128]} | slice | bytes 16769024 | tf_op jit(solution)/shard_map/while/body/eval_jaxpr/slice | solution.py:21
  46.2 12.3 %reshape.150 = s32[1024,2047]{1,0:T(8,128)} reshape(s32[2096128]{0:T(1024)} %slice.292) | data formatting | bytes 16769024 | tf_op jit(solution)/shard_map/while/body/eval_jaxpr/reshape | solution.py:22
  58.5 5.5 %slice.293 = s32[1024,1024]{1,0:T(8,128)} slice(s32[1024,2047]{1,0:T(8,128)} %reshape.150), slice={[0:1024], [1023:2047]} | slice | bytes 8388608 | tf_op jit(solution)/shard_map/while/body/eval_jaxpr/slice | solution.py:22
  65.9 2.0 copy.9
  67.9 3.7 %slice.297 = s32[2096128]{0:T(1024)} slice(s32[2097152]{0:T(1024)S(1)} %bitcast.76), slice={[0:2096128]} | slice | bytes 16769024 | tf_op jit(solution)/shard_map/while/body/eval_jaxpr/slice | solution.py:21
  71.6 12.3 %reshape.151 = s32[1024,2047]{1,0:T(8,128)} reshape(s32[2096128]{0:T(1024)} %slice.297) | data formatting | bytes 16769024 | tf_op jit(solution)/shard_map/while/body/eval_jaxpr/reshape | solution.py:22
  83.9 5.5 %slice.298 = s32[1024,1024]{1,0:T(8,128)} slice(s32[1024,2047]{1,0:T(8,128)} %reshape.151), slice={[0:1024], [1023:2047]} | slice | bytes 8388608 | tf_op jit(solution)/shard_map/while/body/eval_jaxpr/slice | solution.py:22
  89.4 4.5 %gather_fusion = s32[1024]{0:T(1024)S(1)} fusion(s32[1024]{0:T(1024)S(1)} %bitcast.69, s32[1024]{0:T(1024)S(1)} %broadcast_clamp_fusion.1), kind=kCustom, calls=%fused_computation.clone | custom fusion | bytes 12288 | tf_op jit(solution)/shard_map/while/body/eval_jaxpr/jit(_take)/gather | solution.py:14
  95.7 2.0 copy.6
  97.7 4.0 %slice.282 = s32[2096128]{0:T(1024)} slice(s32[2097152]{0:T(1024)S(1)} %bitcast.77), slice={[0:2096128]} | slice | bytes 16769024 | tf_op jit(solution)/shard_map/while/body/eval_jaxpr/slice | solution.py:21
  101.7 12.3 %reshape.148 = s32[1024,2047]{1,0:T(8,128)} reshape(s32[2096128]{0:T(1024)} %slice.282) | data formatting | bytes 16769024 | tf_op jit(solution)/shard_map/while/body/eval_jaxpr/reshape | solution.py:22
  114.0 5.4 %slice.283 = s32[1024,1024]{1,0:T(8,128)} slice(s32[1024,2047]{1,0:T(8,128)} %reshape.148), slice={[0:1024], [1023:2047]} | slice | bytes 8388608 | tf_op jit(solution)/shard_map/while/body/eval_jaxpr/slice | solution.py:22
  121.2 2.0 copy.7
  123.2 3.7 %slice.287 = s32[2096128]{0:T(1024)} slice(s32[2097152]{0:T(1024)S(1)} %bitcast.78), slice={[0:2096128]} | slice | bytes 16769024 | tf_op jit(solution)/shard_map/while/body/eval_jaxpr/slice | solution.py:21
  126.9 12.3 %reshape.149 = s32[1024,2047]{1,0:T(8,128)} reshape(s32[2096128]{0:T(1024)} %slice.287) | data formatting | bytes 16769024 | tf_op jit(solution)/shard_map/while/body/eval_jaxpr/reshape | solution.py:22
  139.2 5.4 %slice.288 = s32[1024,1024]{1,0:T(8,128)} slice(s32[1024,2047]{1,0:T(8,128)} %reshape.149), slice={[0:1024], [1023:2047]} | slice | bytes 8388608 | tf_op jit(solution)/shard_map/while/body/eval_jaxpr/slice | solution.py:22
  145.3 4.3 %broadcast_bitcast_fusion.1 = s32[128,16,8,128]{3,2,1,0:T(8,128)} fusion(s32[2048]{0:T(1024)S(1)} %concatenate.64), kind=kLoop, calls=%fused_computation.21 | loop fusion | bytes 8396800
  150.3 4.3 %broadcast_bitcast_fusion = s32[128,16,8,128]{3,2,1,0:T(8,128)} fusion(s32[2048]{0:T(1024)S(1)} %concatenate.65), kind=kLoop, calls=%fused_computation.20 | loop fusion | bytes 8396800
  155.3 4.3 %broadcast_bitcast_fusion.3 = s32[128,16,8,128]{3,2,1,0:T(8,128)} fusion(s32[2048]{0:T(1024)S(1)} %concatenate.61), kind=kLoop, calls=%fused_computation.23 | loop fusion | bytes 8396800
  160.3 5.3 %broadcast_bitcast_fusion.2 = s32[128,16,8,128]{3,2,1,0:T(8,128)} fusion(s32[2048]{0:T(1024)S(1)} %concatenate.62), kind=kLoop, calls=%fused_computation.22 | loop fusion | bytes 8396800
  165.6 1.2 copy-done.3
  166.8 7.0 %fusion.4 = s32[1,2048]{1,0:T(1,128)S(1)} fusion(s32[1024,1]{0,1:T(1,128)S(1)} %bitcast.88, s32[1024,1024]{1,0:T(8,128)S(1)} %copy-done.3, s32[1024,1024]{1,0:T(8,128)S(1)} %copy-done.2), kind=kOutput, calls=%fused_computation.8 | convolution fusion | flops 6291456 | bytes 8400896 | tf_op jit(solution)/shard_map/while/body/eval_jaxpr/dot_general | solution.py:38
  173.8 6.8 %fusion = s32[1,2048]{1,0:T(1,128)S(1)} fusion(s32[1024,1]{0,1:T(1,128)S(1)} %bitcast.87, s32[1024,1024]{1,0:T(8,128)S(1)} %copy-done.7, s32[1024,1024]{1,0:T(8,128)S(1)} %copy-done.4), kind=kOutput, calls=%fused_computation.4 | convolution fusion | flops 6291456 | bytes 8400896 | tf_op jit(solution)/shard_map/while/body/eval_jaxpr/dot_general | solution.py:38
  182.6 2.4 copy.12
  185.0 3.5 %slice.313 = s32[2096128]{0:T(1024)} slice(s32[2097152]{0:T(1024)S(1)} %bitcast.79), slice={[0:2096128]} | slice | bytes 16769024 | tf_op jit(solution)/shard_map/while/body/eval_jaxpr/slice | solution.py:21
  188.5 12.3 %reshape.154 = s32[1024,2047]{1,0:T(8,128)} reshape(s32[2096128]{0:T(1024)} %slice.313) | data formatting | bytes 16769024 | tf_op jit(solution)/shard_map/while/body/eval_jaxpr/reshape | solution.py:22
  200.8 5.5 %slice.314 = s32[1024,1024]{1,0:T(8,128)} slice(s32[1024,2047]{1,0:T(8,128)} %reshape.154), slice={[0:1024], [1023:2047]} | slice | bytes 8388608 | tf_op jit(solution)/shard_map/while/body/eval_jaxpr/slice | solution.py:22
  206.4 5.4 %copy.13 = s32[128,16,8,128]{3,1,2,0:T(8,128)S(1)} copy(s32[128,16,8,128]{3,2,1,0:T(8,128)} %broadcast_bitcast_fusion) | data formatting | bytes 16777216
  211.8 3.7 %slice.318 = s32[2096128]{0:T(1024)} slice(s32[2097152]{0:T(1024)S(1)} %bitcast.80), slice={[0:2096128]} | slice | bytes 16769024 | tf_op jit(solution)/shard_map/while/body/eval_jaxpr/slice | solution.py:21
  215.4 12.3 %reshape.155 = s32[1024,2047]{1,0:T(8,128)} reshape(s32[2096128]{0:T(1024)} %slice.318) | data formatting | bytes 16769024 | tf_op jit(solution)/shard_map/while/body/eval_jaxpr/reshape | solution.py:22
  227.8 5.5 %slice.319 = s32[1024,1024]{1,0:T(8,128)} slice(s32[1024,2047]{1,0:T(8,128)} %reshape.155), slice={[0:1024], [1023:2047]} | slice | bytes 8388608 | tf_op jit(solution)/shard_map/while/body/eval_jaxpr/slice | solution.py:22
  233.2 5.4 %copy.10 = s32[128,16,8,128]{3,1,2,0:T(8,128)S(1)} copy(s32[128,16,8,128]{3,2,1,0:T(8,128)} %broadcast_bitcast_fusion.3) | data formatting | bytes 16777216
  238.6 3.7 %slice.303 = s32[2096128]{0:T(1024)} slice(s32[2097152]{0:T(1024)S(1)} %bitcast.81), slice={[0:2096128]} | slice | bytes 16769024 | tf_op jit(solution)/shard_map/while/body/eval_jaxpr/slice | solution.py:21
  242.3 12.3 %reshape.152 = s32[1024,2047]{1,0:T(8,128)} reshape(s32[2096128]{0:T(1024)} %slice.303) | data formatting | bytes 16769024 | tf_op jit(solution)/shard_map/while/body/eval_jaxpr/reshape | solution.py:22
  254.6 5.4 %slice.304 = s32[1024,1024]{1,0:T(8,128)} slice(s32[1024,2047]{1,0:T(8,128)} %reshape.152), slice={[0:1024], [1023:2047]} | slice | bytes 8388608 | tf_op jit(solution)/shard_map/while/body/eval_jaxpr/slice | solution.py:22
  260.0 5.4 %copy.11 = s32[128,16,8,128]{3,1,2,0:T(8,128)S(1)} copy(s32[128,16,8,128]{3,2,1,0:T(8,128)} %broadcast_bitcast_fusion.2) | data formatting | bytes 16777216
  265.4 3.7 %slice.308 = s32[2096128]{0:T(1024)} slice(s32[2097152]{0:T(1024)S(1)} %bitcast.82), slice={[0:2096128]} | slice | bytes 16769024 | tf_op jit(solution)/shard_map/while/body/eval_jaxpr/slice | solution.py:21
  269.2 12.3 %reshape.153 = s32[1024,2047]{1,0:T(8,128)} reshape(s32[2096128]{0:T(1024)} %slice.308) | data formatting | bytes 16769024 | tf_op jit(solution)/shard_map/while/body/eval_jaxpr/reshape | solution.py:22
  281.5 5.4 %slice.309 = s32[1024,1024]{1,0:T(8,128)} slice(s32[1024,2047]{1,0:T(8,128)} %reshape.153), slice={[0:1024], [1023:2047]} | slice | bytes 8388608 | tf_op jit(solution)/shard_map/while/body/eval_jaxpr/slice | solution.py:22
  287.9 4.5 %gather_fusion.2 = s32[1024]{0:T(1024)S(1)} fusion(s32[1024]{0:T(1024)S(1)} %bitcast.71, s32[1024]{0:T(1024)S(1)} %broadcast_clamp_fusion.1), kind=kCustom, calls=%fused_computation.2.clone | custom fusion | bytes 12288 | tf_op jit(solution)/shard_map/while/body/eval_jaxpr/jit(_take)/gather | solution.py:14
  292.5 4.5 %gather_fusion.3 = s32[1024]{0:T(1024)S(1)} fusion(s32[1024]{0:T(1024)S(1)} %get-tuple-element.68, s32[1024]{0:T(1024)S(1)} %get-tuple-element.73), kind=kCustom, calls=%fused_computation.3.clone | custom fusion | bytes 12288 | tf_op jit(solution)/shard_map/while/body/eval_jaxpr/jit(_take)/gather | solution.py:14
  297.0 4.5 %gather_fusion.1 = s32[1024]{0:T(1024)S(1)} fusion(s32[1024]{0:T(1024)S(1)} %get-tuple-element.67, s32[1024]{0:T(1024)S(1)} %get-tuple-element.73), kind=kCustom, calls=%fused_computation.1.clone | custom fusion | bytes 12288 | tf_op jit(solution)/shard_map/while/body/eval_jaxpr/jit(_take)/gather | solution.py:14
  301.6 9.5 %fusion.12 = s32[1,2048]{1,0:T(1,128)S(1)} fusion(s32[1024,1]{0,1:T(1,128)S(1)} %bitcast.90, s32[1024,1024]{1,0:T(8,128)} %slice.319, s32[1024,1024]{1,0:T(8,128)} %slice.314), kind=kOutput, calls=%fused_computation.16 | convolution fusion | flops 6291456 | bytes 8400896 | tf_op jit(solution)/shard_map/while/body/eval_jaxpr/dot_general | solution.py:38
  311.1 6.8 %fusion.8 = s32[1,2048]{1,0:T(1,128)S(1)} fusion(s32[1024,1]{0,1:T(1,128)S(1)} %bitcast.89, s32[1024,1024]{1,0:T(8,128)S(1)} %copy-done.6, s32[1024,1024]{1,0:T(8,128)S(1)} %copy-done.5), kind=kOutput, calls=%fused_computation.12 | convolution fusion | flops 6291456 | bytes 8400896 | tf_op jit(solution)/shard_map/while/body/eval_jaxpr/dot_general | solution.py:38
  (58 shorter events, 9.0 us)
Async XLA Ops:
  6.5 0.9 copy-start
  6.5 280.4 %all-reduce.3.cloned.1.call-start = ((), (), s32[]{:S(2)}) async-start(), calls=%async_computation | async-start | bytes 262144 | tf_op jit(solution)/shard_map/psum | solution.py:74
  83.9 5.5 %copy-start.8 = (s32[2,1024]{1,0:T(2,128)S(1)}, s32[2,1024]{1,0:T(2,128)}, u32[]{:S(2)}) copy-start(s32[2,1024]{1,0:T(2,128)} %param.10) | copy-start | bytes 24580
  160.3 5.3 %copy-start.2 = (s32[1024,1024]{1,0:T(8,128)S(1)}, s32[1024,1024]{1,0:T(8,128)}, u32[]{:S(2)}) copy-start(s32[1024,1024]{1,0:T(8,128)} %slice.293) | copy-start | bytes 12582916
  160.3 6.5 %copy-start.3 = (s32[1024,1024]{1,0:T(8,128)S(1)}, s32[1024,1024]{1,0:T(8,128)}, u32[]{:S(2)}) copy-start(s32[1024,1024]{1,0:T(8,128)} %slice.298) | copy-start | bytes 12582916
  160.3 13.5 %copy-start.4 = (s32[1024,1024]{1,0:T(8,128)S(1)}, s32[1024,1024]{1,0:T(8,128)}, u32[]{:S(2)}) copy-start(s32[1024,1024]{1,0:T(8,128)} %slice.283) | copy-start | bytes 12582916
  160.3 13.5 %copy-start.7 = (s32[1024,1024]{1,0:T(8,128)S(1)}, s32[1024,1024]{1,0:T(8,128)}, u32[]{:S(2)}) copy-start(s32[1024,1024]{1,0:T(8,128)} %slice.288) | copy-start | bytes 12582916
  166.8 15.7 %slice-start = ((s8[8388608]{0:T(1024)(128)(4,1)}), s8[4194304]{0:T(1024)(128)(4,1)S(1)}, s32[]{:S(2)}) async-start(s8[8388608]{0:T(1024)(128)(4,1)} %bitcast.73), calls=%async_computation.1 | async-start | bytes 8388608
  173.8 8.7 %slice-start.1 = ((s8[8388608]{0:T(1024)(128)(4,1)}), s8[4194304]{0:T(1024)(128)(4,1)S(1)}, s32[]{:S(2)}) async-start(s8[8388608]{0:T(1024)(128)(4,1)} %bitcast.73), calls=%async_computation.2 | async-start | bytes 8388608
  301.5 9.6 %copy-start.5 = (s32[1024,1024]{1,0:T(8,128)S(1)}, s32[1024,1024]{1,0:T(8,128)}, u32[]{:S(2)}) copy-start(s32[1024,1024]{1,0:T(8,128)} %slice.304) | copy-start | bytes 12582916
  301.6 9.6 %copy-start.6 = (s32[1024,1024]{1,0:T(8,128)S(1)}, s32[1024,1024]{1,0:T(8,128)}, u32[]{:S(2)}) copy-start(s32[1024,1024]{1,0:T(8,128)} %slice.309) | copy-start | bytes 12582916
  301.6 17.0 %copy-start.1 = (s32[16,2048]{1,0:T(8,128)S(1)}, s32[16,2048]{1,0:T(8,128)}, u32[]{:S(2)}) copy-start(s32[16,2048]{1,0:T(8,128)} %param.7) | copy-start | bytes 393220
Sparse Core Ops, SparseCore 0:
  10.9 91.1 all-reduce.2
where the time goes:
time: 330 us; the launch traced here: 326 us
  local copies, waits for them, and re-layouts  244 us (74%)
  matrix products  31.6 us (10%)
  blocking collectives  24.2 us (7%)
  between operations  23.8 us (7%)
    reshape x8, local copies, waits for them, and re-layouts, toeplitz(): tiled_rows.reshape(cycle_width, 2 * cycle_width - 1)  98.5 us
    unnamed x38, local copies, waits for them, and re-layouts  51 us
    slice x8, local copies, waits for them, and re-layouts, toeplitz(): tiled_rows.reshape(cycle_width, 2 * cycle_width - 1)  43.7 us
    dot_general x4, matrix products, switch_section(): jnp.dot(digit_row[None, :], matrix, preferred_element_type=jnp.int32)[0]  30 us
    slice x8, local copies, waits for them, and re-layouts, toeplitz(): jnp.tile(shifted, cycle_width)[:cycle_width * (2 * cycle_width - 1)]  29.8 us
    all_gather x1, blocking collectives, on_device(): key_table = lax.all_gather(key_rows, 'col', axis=1, tiled=True)  24.2 us
    gather x4, local copies, waits for them, and re-layouts, automorph(): picked = jnp.take(polynomial, source % cycle_width, axis=0)  18.1 us
  transfers between devices with their start and end apart: 1, of which 0 were waited for; matrix products, arithmetic and copies ran while one was open for 74% of the time, Pallas kernels for 0%

commit v1 on v0

--- a/solution.py
+++ b/solution.py
@@ -65,7 +65,7 @@
     cycle_width = hint.shape[1]
     poly_count = hint.shape[0]
     slot_count = assignment.shape[0] // lax.axis_size("col")
-    key_table = lax.all_gather(key_rows, "col", axis=1, tiled=True)
+    key_table = jnp.concatenate(lax.all_gather(key_rows, axis_name="col"), 1)
     partial_value = jnp.dot(queries, database, preferred_element_type=jnp.int32)
     owned_slots = lax.dynamic_slice_in_dim(
         assignment, lax.axis_index("col") * slot_count, slot_count

time: 330 us -> 330 us (level)
  no operation moved by 1% of the time
where the time goes in v1:
time: 330 us; the launch traced here: 326 us
  local copies, waits for them, and re-layouts  244 us (74%)
  matrix products  31.6 us (10%)
  blocking collectives  24.2 us (7%)
  between operations  23.8 us (7%)
    reshape x8, local copies, waits for them, and re-layouts, toeplitz(): tiled_rows.reshape(cycle_width, 2 * cycle_width - 1)  98.5 us
    unnamed x38, local copies, waits for them, and re-layouts  51 us
    slice x8, local copies, waits for them, and re-layouts, toeplitz(): tiled_rows.reshape(cycle_width, 2 * cycle_width - 1)  43.7 us
    dot_general x4, matrix products, switch_section(): jnp.dot(digit_row[None, :], matrix, preferred_element_type=jnp.int32)[0]  30 us
    slice x8, local copies, waits for them, and re-layouts, toeplitz(): jnp.tile(shifted, cycle_width)[:cycle_width * (2 * cycle_width - 1)]  29.8 us
    all_gather x1, blocking collectives, on_device(): key_table = jnp.concatenate(lax.all_gather(key_rows, axis_name='col'), 1)  24.2 us
    gather x4, local copies, waits for them, and re-layouts, automorph(): picked = jnp.take(polynomial, source % cycle_width, axis=0)  18.1 us
  transfers between devices with their start and end apart: 1, of which 0 were waited for; matrix products, arithmetic and copies ran while one was open for 74% of the time, Pallas kernels for 0%

profile of v1, /device:TPU:0, one launch (start us, length us, event | category | flops | bytes accessed | tf_op | source)
XLA Modules:
  0.0 325.9 jit_solution(15908655947112434860)
XLA Ops:
  7.4 1.6 and_convert_fusion.1
  9.1 1.2 dynamic_slice.19
  12.9 24.2 %all-gather = s32[128,512]{1,0:T(8,128)S(1)} all-gather(s32[8,512]{1,0:T(8,128)} %param.9), channel_id=2, replica_groups=mesh['grp'=2,'col'=16] {'col'}, dimensions={0}, use_global_device_ids=true | all-gather | bytes 278528 | tf_op jit(solution)/shard_map/all_gather | solution.py:68
  40.4 2.0 copy.8
  42.4 3.7 %slice.292 = s32[2096128]{0:T(1024)} slice(s32[2097152]{0:T(1024)S(1)} %bitcast.80), slice={[0:2096128]} | slice | bytes 16769024 | tf_op jit(solution)/shard_map/while/body/eval_jaxpr/slice | solution.py:21
  46.2 12.3 %reshape.158 = s32[1024,2047]{1,0:T(8,128)} reshape(s32[2096128]{0:T(1024)} %slice.292) | data formatting | bytes 16769024 | tf_op jit(solution)/shard_map/while/body/eval_jaxpr/reshape | solution.py:22
  58.5 5.5 %slice.293 = s32[1024,1024]{1,0:T(8,128)} slice(s32[1024,2047]{1,0:T(8,128)} %reshape.158), slice={[0:1024], [1023:2047]} | slice | bytes 8388608 | tf_op jit(solution)/shard_map/while/body/eval_jaxpr/slice | solution.py:22
  65.9 2.0 copy.9
  67.9 3.7 %slice.297 = s32[2096128]{0:T(1024)} slice(s32[2097152]{0:T(1024)S(1)} %bitcast.81), slice={[0:2096128]} | slice | bytes 16769024 | tf_op jit(solution)/shard_map/while/body/eval_jaxpr/slice | solution.py:21
  71.6 12.3 %reshape.159 = s32[1024,2047]{1,0:T(8,128)} reshape(s32[2096128]{0:T(1024)} %slice.297) | data formatting | bytes 16769024 | tf_op jit(solution)/shard_map/while/body/eval_jaxpr/reshape | solution.py:22
  83.9 5.5 %slice.298 = s32[1024,1024]{1,0:T(8,128)} slice(s32[1024,2047]{1,0:T(8,128)} %reshape.159), slice={[0:1024], [1023:2047]} | slice | bytes 8388608 | tf_op jit(solution)/shard_map/while/body/eval_jaxpr/slice | solution.py:22
  89.4 4.5 %gather_fusion = s32[1024]{0:T(1024)S(1)} fusion(s32[1024]{0:T(1024)S(1)} %bitcast.74, s32[1024]{0:T(1024)S(1)} %broadcast_clamp_fusion.1), kind=kCustom, calls=%fused_computation.clone | custom fusion | bytes 12288 | tf_op jit(solution)/shard_map/while/body/eval_jaxpr/jit(_take)/gather | solution.py:14
  95.7 2.0 copy.6
  97.7 4.0 %slice.282 = s32[2096128]{0:T(1024)} slice(s32[2097152]{0:T(1024)S(1)} %bitcast.82), slice={[0:2096128]} | slice | bytes 16769024 | tf_op jit(solution)/shard_map/while/body/eval_jaxpr/slice | solution.py:21
  101.7 12.3 %reshape.156 = s32[1024,2047]{1,0:T(8,128)} reshape(s32[2096128]{0:T(1024)} %slice.282) | data formatting | bytes 16769024 | tf_op jit(solution)/shard_map/while/body/eval_jaxpr/reshape | solution.py:22
  114.0 5.4 %slice.283 = s32[1024,1024]{1,0:T(8,128)} slice(s32[1024,2047]{1,0:T(8,128)} %reshape.156), slice={[0:1024], [1023:2047]} | slice | bytes 8388608 | tf_op jit(solution)/shard_map/while/body/eval_jaxpr/slice | solution.py:22
  121.2 2.0 copy.7
  123.2 3.7 %slice.287 = s32[2096128]{0:T(1024)} slice(s32[2097152]{0:T(1024)S(1)} %bitcast.83), slice={[0:2096128]} | slice | bytes 16769024 | tf_op jit(solution)/shard_map/while/body/eval_jaxpr/slice | solution.py:21
  126.9 12.3 %reshape.157 = s32[1024,2047]{1,0:T(8,128)} reshape(s32[2096128]{0:T(1024)} %slice.287) | data formatting | bytes 16769024 | tf_op jit(solution)/shard_map/while/body/eval_jaxpr/reshape | solution.py:22
  139.2 5.4 %slice.288 = s32[1024,1024]{1,0:T(8,128)} slice(s32[1024,2047]{1,0:T(8,128)} %reshape.157), slice={[0:1024], [1023:2047]} | slice | bytes 8388608 | tf_op jit(solution)/shard_map/while/body/eval_jaxpr/slice | solution.py:22
  145.3 4.3 %broadcast_bitcast_fusion.1 = s32[128,16,8,128]{3,2,1,0:T(8,128)} fusion(s32[2048]{0:T(1024)S(1)} %concatenate.64), kind=kLoop, calls=%fused_computation.21 | loop fusion | bytes 8396800
  150.3 4.3 %broadcast_bitcast_fusion = s32[128,16,8,128]{3,2,1,0:T(8,128)} fusion(s32[2048]{0:T(1024)S(1)} %concatenate.65), kind=kLoop, calls=%fused_computation.20 | loop fusion | bytes 8396800
  155.3 4.3 %broadcast_bitcast_fusion.3 = s32[128,16,8,128]{3,2,1,0:T(8,128)} fusion(s32[2048]{0:T(1024)S(1)} %concatenate.61), kind=kLoop, calls=%fused_computation.23 | loop fusion | bytes 8396800
  160.3 5.3 %broadcast_bitcast_fusion.2 = s32[128,16,8,128]{3,2,1,0:T(8,128)} fusion(s32[2048]{0:T(1024)S(1)} %concatenate.62), kind=kLoop, calls=%fused_computation.22 | loop fusion | bytes 8396800
  165.6 1.2 copy-done.3
  166.8 7.0 %fusion.4 = s32[1,2048]{1,0:T(1,128)S(1)} fusion(s32[1024,1]{0,1:T(1,128)S(1)} %bitcast.94, s32[1024,1024]{1,0:T(8,128)S(1)} %copy-done.3, s32[1024,1024]{1,0:T(8,128)S(1)} %copy-done.2), kind=kOutput, calls=%fused_computation.8 | convolution fusion | flops 6291456 | bytes 8400896 | tf_op jit(solution)/shard_map/while/body/eval_jaxpr/dot_general | solution.py:38
  173.8 6.8 %fusion = s32[1,2048]{1,0:T(1,128)S(1)} fusion(s32[1024,1]{0,1:T(1,128)S(1)} %bitcast.93, s32[1024,1024]{1,0:T(8,128)S(1)} %copy-done.7, s32[1024,1024]{1,0:T(8,128)S(1)} %copy-done.4), kind=kOutput, calls=%fused_computation.4 | convolution fusion | flops 6291456 | bytes 8400896 | tf_op jit(solution)/shard_map/while/body/eval_jaxpr/dot_general | solution.py:38
  182.6 2.4 copy.12
  185.0 3.5 %slice.313 = s32[2096128]{0:T(1024)} slice(s32[2097152]{0:T(1024)S(1)} %bitcast.84), slice={[0:2096128]} | slice | bytes 16769024 | tf_op jit(solution)/shard_map/while/body/eval_jaxpr/slice | solution.py:21
  188.5 12.3 %reshape.162 = s32[1024,2047]{1,0:T(8,128)} reshape(s32[2096128]{0:T(1024)} %slice.313) | data formatting | bytes 16769024 | tf_op jit(solution)/shard_map/while/body/eval_jaxpr/reshape | solution.py:22
  200.8 5.5 %slice.314 = s32[1024,1024]{1,0:T(8,128)} slice(s32[1024,2047]{1,0:T(8,128)} %reshape.162), slice={[0:1024], [1023:2047]} | slice | bytes 8388608 | tf_op jit(solution)/shard_map/while/body/eval_jaxpr/slice | solution.py:22
  206.4 5.4 %copy.13 = s32[128,16,8,128]{3,1,2,0:T(8,128)S(1)} copy(s32[128,16,8,128]{3,2,1,0:T(8,128)} %broadcast_bitcast_fusion) | data formatting | bytes 16777216
  211.8 3.7 %slice.318 = s32[2096128]{0:T(1024)} slice(s32[2097152]{0:T(1024)S(1)} %bitcast.85), slice={[0:2096128]} | slice | bytes 16769024 | tf_op jit(solution)/shard_map/while/body/eval_jaxpr/slice | solution.py:21
  215.4 12.3 %reshape.163 = s32[1024,2047]{1,0:T(8,128)} reshape(s32[2096128]{0:T(1024)} %slice.318) | data formatting | bytes 16769024 | tf_op jit(solution)/shard_map/while/body/eval_jaxpr/reshape | solution.py:22
  227.8 5.5 %slice.319 = s32[1024,1024]{1,0:T(8,128)} slice(s32[1024,2047]{1,0:T(8,128)} %reshape.163), slice={[0:1024], [1023:2047]} | slice | bytes 8388608 | tf_op jit(solution)/shard_map/while/body/eval_jaxpr/slice | solution.py:22
  233.2 5.4 %copy.10 = s32[128,16,8,128]{3,1,2,0:T(8,128)S(1)} copy(s32[128,16,8,128]{3,2,1,0:T(8,128)} %broadcast_bitcast_fusion.3) | data formatting | bytes 16777216
  238.6 3.7 %slice.303 = s32[2096128]{0:T(1024)} slice(s32[2097152]{0:T(1024)S(1)} %bitcast.86), slice={[0:2096128]} | slice | bytes 16769024 | tf_op jit(solution)/shard_map/while/body/eval_jaxpr/slice | solution.py:21
  242.3 12.3 %reshape.160 = s32[1024,2047]{1,0:T(8,128)} reshape(s32[2096128]{0:T(1024)} %slice.303) | data formatting | bytes 16769024 | tf_op jit(solution)/shard_map/while/body/eval_jaxpr/reshape | solution.py:22
  254.6 5.4 %slice.304 = s32[1024,1024]{1,0:T(8,128)} slice(s32[1024,2047]{1,0:T(8,128)} %reshape.160), slice={[0:1024], [1023:2047]} | slice | bytes 8388608 | tf_op jit(solution)/shard_map/while/body/eval_jaxpr/slice | solution.py:22
  260.0 5.4 %copy.11 = s32[128,16,8,128]{3,1,2,0:T(8,128)S(1)} copy(s32[128,16,8,128]{3,2,1,0:T(8,128)} %broadcast_bitcast_fusion.2) | data formatting | bytes 16777216
  265.4 3.7 %slice.308 = s32[2096128]{0:T(1024)} slice(s32[2097152]{0:T(1024)S(1)} %bitcast.87), slice={[0:2096128]} | slice | bytes 16769024 | tf_op jit(solution)/shard_map/while/body/eval_jaxpr/slice | solution.py:21
  269.2 12.3 %reshape.161 = s32[1024,2047]{1,0:T(8,128)} reshape(s32[2096128]{0:T(1024)} %slice.308) | data formatting | bytes 16769024 | tf_op jit(solution)/shard_map/while/body/eval_jaxpr/reshape | solution.py:22
  281.5 5.4 %slice.309 = s32[1024,1024]{1,0:T(8,128)} slice(s32[1024,2047]{1,0:T(8,128)} %reshape.161), slice={[0:1024], [1023:2047]} | slice | bytes 8388608 | tf_op jit(solution)/shard_map/while/body/eval_jaxpr/slice | solution.py:22
  287.9 4.5 %gather_fusion.2 = s32[1024]{0:T(1024)S(1)} fusion(s32[1024]{0:T(1024)S(1)} %bitcast.76, s32[1024]{0:T(1024)S(1)} %broadcast_clamp_fusion.1), kind=kCustom, calls=%fused_computation.2.clone | custom fusion | bytes 12288 | tf_op jit(solution)/shard_map/while/body/eval_jaxpr/jit(_take)/gather | solution.py:14
  292.5 4.5 %gather_fusion.3 = s32[1024]{0:T(1024)S(1)} fusion(s32[1024]{0:T(1024)S(1)} %get-tuple-element.68, s32[1024]{0:T(1024)S(1)} %get-tuple-element.73), kind=kCustom, calls=%fused_computation.3.clone | custom fusion | bytes 12288 | tf_op jit(solution)/shard_map/while/body/eval_jaxpr/jit(_take)/gather | solution.py:14
  297.0 4.5 %gather_fusion.1 = s32[1024]{0:T(1024)S(1)} fusion(s32[1024]{0:T(1024)S(1)} %get-tuple-element.67, s32[1024]{0:T(1024)S(1)} %get-tuple-element.73), kind=kCustom, calls=%fused_computation.1.clone | custom fusion | bytes 12288 | tf_op jit(solution)/shard_map/while/body/eval_jaxpr/jit(_take)/gather | solution.py:14
  301.6 9.5 %fusion.12 = s32[1,2048]{1,0:T(1,128)S(1)} fusion(s32[1024,1]{0,1:T(1,128)S(1)} %bitcast.96, s32[1024,1024]{1,0:T(8,128)} %slice.319, s32[1024,1024]{1,0:T(8,128)} %slice.314), kind=kOutput, calls=%fused_computation.16 | convolution fusion | flops 6291456 | bytes 8400896 | tf_op jit(solution)/shard_map/while/body/eval_jaxpr/dot_general | solution.py:38
  311.1 6.8 %fusion.8 = s32[1,2048]{1,0:T(1,128)S(1)} fusion(s32[1024,1]{0,1:T(1,128)S(1)} %bitcast.95, s32[1024,1024]{1,0:T(8,128)S(1)} %copy-done.6, s32[1024,1024]{1,0:T(8,128)S(1)} %copy-done.5), kind=kOutput, calls=%fused_computation.12 | convolution fusion | flops 6291456 | bytes 8400896 | tf_op jit(solution)/shard_map/while/body/eval_jaxpr/dot_general | solution.py:38
  (58 shorter events, 9.0 us)
Async XLA Ops:
  6.5 0.9 copy-start
  6.5 280.4 %all-reduce.3.cloned.1.call-start = ((), (), s32[]{:S(2)}) async-start(), calls=%async_computation | async-start | bytes 262144 | tf_op jit(solution)/shard_map/psum | solution.py:74
  83.9 5.5 %copy-start.8 = (s32[2,1024]{1,0:T(2,128)S(1)}, s32[2,1024]{1,0:T(2,128)}, u32[]{:S(2)}) copy-start(s32[2,1024]{1,0:T(2,128)} %param.10) | copy-start | bytes 24580
  160.3 5.3 %copy-start.2 = (s32[1024,1024]{1,0:T(8,128)S(1)}, s32[1024,1024]{1,0:T(8,128)}, u32[]{:S(2)}) copy-start(s32[1024,1024]{1,0:T(8,128)} %slice.293) | copy-start | bytes 12582916
  160.3 6.5 %copy-start.3 = (s32[1024,1024]{1,0:T(8,128)S(1)}, s32[1024,1024]{1,0:T(8,128)}, u32[]{:S(2)}) copy-start(s32[1024,1024]{1,0:T(8,128)} %slice.298) | copy-start | bytes 12582916
  160.3 13.5 %copy-start.4 = (s32[1024,1024]{1,0:T(8,128)S(1)}, s32[1024,1024]{1,0:T(8,128)}, u32[]{:S(2)}) copy-start(s32[1024,1024]{1,0:T(8,128)} %slice.283) | copy-start | bytes 12582916
  160.3 13.5 %copy-start.7 = (s32[1024,1024]{1,0:T(8,128)S(1)}, s32[1024,1024]{1,0:T(8,128)}, u32[]{:S(2)}) copy-start(s32[1024,1024]{1,0:T(8,128)} %slice.288) | copy-start | bytes 12582916
  166.8 15.7 %slice-start = ((s8[8388608]{0:T(1024)(128)(4,1)}), s8[4194304]{0:T(1024)(128)(4,1)S(1)}, s32[]{:S(2)}) async-start(s8[8388608]{0:T(1024)(128)(4,1)} %bitcast.78), calls=%async_computation.1 | async-start | bytes 8388608
  173.8 8.7 %slice-start.1 = ((s8[8388608]{0:T(1024)(128)(4,1)}), s8[4194304]{0:T(1024)(128)(4,1)S(1)}, s32[]{:S(2)}) async-start(s8[8388608]{0:T(1024)(128)(4,1)} %bitcast.78), calls=%async_computation.2 | async-start | bytes 8388608
  301.5 9.6 %copy-start.5 = (s32[1024,1024]{1,0:T(8,128)S(1)}, s32[1024,1024]{1,0:T(8,128)}, u32[]{:S(2)}) copy-start(s32[1024,1024]{1,0:T(8,128)} %slice.304) | copy-start | bytes 12582916
  301.6 9.6 %copy-start.6 = (s32[1024,1024]{1,0:T(8,128)S(1)}, s32[1024,1024]{1,0:T(8,128)}, u32[]{:S(2)}) copy-start(s32[1024,1024]{1,0:T(8,128)} %slice.309) | copy-start | bytes 12582916
  301.6 17.0 %copy-start.1 = (s32[16,2048]{1,0:T(8,128)S(1)}, s32[16,2048]{1,0:T(8,128)}, u32[]{:S(2)}) copy-start(s32[16,2048]{1,0:T(8,128)} %param.7) | copy-start | bytes 393220
Sparse Core Ops, SparseCore 0:
  10.9 91.1 all-reduce.2
